TPU v7x, 32 devices: a whole 2x2x4 slice. The times are simulated.
32 devices in a mesh: smp: 8 (over z, y), par: 4 (over x, core).
Axes of the slice: x: 2, y: 2, z: 4, core: 2. Of those that a mesh axis runs over, the one named last changes fastest.
Arguments:
- derivatives: bfloat16 [640, 2048], P('smp', 'par'), may hold values from -40 to 40
- epsilon: float32 [640], P('smp'), may hold values from -6 to 6
Outputs:
- gram_tile: float32 [640, 640], P('smp', 'par')
- update: float32 [2048], P('par')
All inputs are finite; a program needn't handle non-finite values.
Results may differ from a plain program's by a relative error of at most 0.003.
Values may be sent and summed in bfloat16 or wider, within the bound.
No kernel may reach another device: no remote copies, remote signals or barrier semaphores. Data moves between devices by JAX's collectives and lax.ppermute only.
A program may use at most 64 MiB of HBM per device.

v0:
```python
import math
import jax
import jax.numpy as jnp
from jax import lax
from jax.sharding import PartitionSpec as P


def shards(derivatives, epsilon):
    total_rows = derivatives.shape[0] * lax.axis_size("smp")
    factor = 1.0 / math.sqrt(total_rows)
    totals = lax.psum(jnp.sum(derivatives.astype(jnp.float32), axis=0), "smp")
    column_mean = totals / total_rows

    def center(values):
        return ((values.astype(jnp.float32) - column_mean) * factor).astype(jnp.bfloat16)

    own_rows = center(derivatives)
    partial_terms = jnp.dot(
        own_rows,
        center(lax.all_gather(derivatives, "smp", axis=0, tiled=True)).T,
        preferred_element_type=jnp.float32,
    )
    gram_tile = lax.psum_scatter(partial_terms, "par", scatter_dimension=1, tiled=True)
    local_sum = jnp.dot(epsilon, own_rows.astype(jnp.float32), precision=lax.Precision.HIGHEST)
    update = lax.psum(local_sum, "smp")
    return (gram_tile, update)


def solution(mesh):
    in_specs = (P("smp", "par"), P("smp"))
    out_specs = (P("smp", "par"), P("par"))
    return jax.shard_map(shards, mesh=mesh, in_specs=in_specs, out_specs=out_specs, check_vma=False)
```

profile of v0, /device:TPU:0, one launch (start us, length us, event | category | flops | bytes accessed | tf_op | source)
XLA Modules:
  0.0 90.6 jit_solution(17457802798909675866)
XLA Ops:
  7.2 0.0 copy-start
  7.2 0.0 copy-start.1
  7.2 0.0 reduce-scatter.4.cloned.1.call-start
  7.2 0.9 %convert_reduce_fusion = f32[512]{0:T(512)S(1)} fusion(bf16[80,512]{1,0:T(8,128)(2,1)} %param.2), kind=kLoop, calls=%fused_computation.5 | loop fusion | flops 81408 | bytes 83968 | tf_op jit(solution)/shard_map/reduce_sum | solution.py:11
  8.2 33.6 %all_gather.3 = bf16[640,512]{1,0:T(8,128)(2,1)S(1)} all-gather(bf16[80,512]{1,0:T(8,128)(2,1)} %param.2), channel_id=1, replica_groups=mesh['smp'=8,'par'=4] {'smp'}, dimensions={0}, use_global_device_ids=true | all-gather | bytes 737280 | tf_op jit(solution)/shard_map/all_gather | solution.py:20
  41.8 21.4 %psum.14 = f32[512]{0:T(512)S(1)} all-reduce(f32[512]{0:T(512)S(1)} %convert_reduce_fusion), channel_id=1, replica_groups=mesh['smp'=8,'par'=4] {'smp'}, use_global_device_ids=true, to_apply=%region_1.0 | all-reduce | flops 512 | bytes 4096 | tf_op jit(solution)/shard_map/psum | solution.py:11
  63.2 0.0 copy-done.1
  63.2 1.1 %convolution_bitcast_fusion = f32[640,80]{1,0:T(8,128)} fusion(bf16[640,512]{1,0:T(8,128)(2,1)S(1)} %all_gather.3, f32[512]{0:T(512)S(1)} %broadcast_multiply_fusion, bf16[80,512]{1,0:T(8,128)(2,1)S(1)} %copy-done.1), kind=kOutput, calls=%fused_computation.1 | convolution fusion | flops 53903360 | bytes 944128
  64.3 0.0 reduce-scatter.4.cloned.1.call-update
  64.3 0.0 copy-done
  64.3 0.2 fusion.4
  64.5 17.7 %psum.15 = f32[512]{0:T(512)} all-reduce(f32[512]{0:T(512)S(1)} %bitcast.8), channel_id=1, replica_groups=mesh['smp'=8,'par'=4] {'smp'}, use_global_device_ids=true, to_apply=%region_3.0 | all-reduce | flops 512 | bytes 4096 | tf_op jit(solution)/shard_map/psum | solution.py:25
  82.2 0.0 reduce-scatter.4.cloned.1.call-done
  82.2 1.6 %copy.5 = f32[80,160]{1,0:T(8,128)} copy(f32[80,160]{0,1:T(8,128)} %bitcast.7) | data formatting | bytes 102400
  (1 shorter events, 0.0 us)
Async XLA Ops:
  7.2 57.2 %copy-start = (f32[80]{0:T(128)S(1)}, f32[80]{0:T(128)}, u32[]{:S(2)}) copy-start(f32[80]{0:T(128)} %param.3) | copy-start | bytes 964
  7.2 56.1 %copy-start.1 = (bf16[80,512]{1,0:T(8,128)(2,1)S(1)}, bf16[80,512]{1,0:T(8,128)(2,1)}, u32[]{:S(2)}) copy-start(bf16[80,512]{1,0:T(8,128)(2,1)} %param.2) | copy-start | bytes 245764
  7.2 75.0 %reduce-scatter.4.cloned.1.call-start = ((), (), s32[]{:S(2)}) async-start(), calls=%async_computation.1 | async-start | bytes 409600
Sparse Core Ops, SparseCore 0:
  64.4 17.6 reduce-scatter.3
where the time goes:
time: 90.9 us; the launch traced here: 90.6 us
  blocking collectives  72.8 us (80%)
  between operations  14.1 us (16%)
  local copies, waits for them, and re-layouts  1.62 us (2%)
  matrix products  1.21 us (1%)
  other arithmetic  0.94 us (1%)
    all_gather x1, blocking collectives, shards(): lax.all_gather(derivatives, 'smp', axis=0, tiled=True)  33.6 us
    psum x1, blocking collectives, shards(): totals = lax.psum(jnp.sum(derivatives.astype(jnp.float32), axis=0), 'smp')  21.4 us
    psum x1, blocking collectives, shards(): update = lax.psum(local_sum, 'smp')  17.7 us
  transfers between devices with their start and end apart: 1, of which 0 were waited for; matrix products, arithmetic and copies ran while one was open for 0% of the time, Pallas kernels for 0%

commit v1 on v0

--- a/solution.py
+++ b/solution.py
@@ -22,7 +22,7 @@
     )
     gram_tile = lax.psum_scatter(partial_terms, "par", scatter_dimension=1, tiled=True)
     local_sum = jnp.dot(epsilon, own_rows.astype(jnp.float32), precision=lax.Precision.HIGHEST)
-    update = lax.psum(local_sum, "smp")
+    update = jnp.sum(lax.all_gather(local_sum, "smp"), axis=0)
     return (gram_tile, update)
 
 

time: 90.9 us -> 99.9 us (1.099)
  blocking collectives: 72.8 us -> 81.2 us
    all_gather x0 -> x1, blocking collectives: none -> 26.1 us  [shards(): update = jnp.sum(lax.all_gather(local_sum, 'smp'), axis=0)]
    psum x1 -> x0, blocking collectives: 17.7 us -> none  [shards(): update = lax.psum(local_sum, 'smp')]
  transfers between devices with their start and end apart: 1 -> 1, of which waited for: 0 -> 0; matrix products, arithmetic and copies ran while one was open for 0% -> 1% of each run, Pallas kernels for 0% -> 0%
where the time goes in v1:
time: 99.9 us; the launch traced here: 99.7 us
  blocking collectives  81.2 us (81%)
  between operations  14.1 us (14%)
  local copies, waits for them, and re-layouts  1.62 us (2%)
  other arithmetic  1.55 us (2%)
  matrix products  1.21 us (1%)
    all_gather x1, blocking collectives, shards(): lax.all_gather(derivatives, 'smp', axis=0, tiled=True)  33.6 us
    all_gather x1, blocking collectives, shards(): update = jnp.sum(lax.all_gather(local_sum, 'smp'), axis=0)  26.1 us
    psum x1, blocking collectives, shards(): totals = lax.psum(jnp.sum(derivatives.astype(jnp.float32), axis=0), 'smp')  21.4 us
  transfers between devices with their start and end apart: 1, of which 0 were waited for; matrix products, arithmetic and copies ran while one was open for 1% of the time, Pallas kernels for 0%

profile of v1, /device:TPU:0, one launch (start us, length us, event | category | flops | bytes accessed | tf_op | source)
XLA Modules:
  0.0 99.7 jit_solution(472637263263299209)
XLA Ops:
  7.2 0.0 copy-start
  7.2 0.0 copy-start.1
  7.2 0.0 reduce-scatter.4.cloned.1.call-start
  7.2 0.9 convert_reduce_fusion
  8.2 33.6 %all_gather.9 = bf16[640,512]{1,0:T(8,128)(2,1)S(1)} all-gather(bf16[80,512]{1,0:T(8,128)(2,1)} %param.2), channel_id=1, replica_groups=mesh['smp'=8,'par'=4] {'smp'}, dimensions={0}, use_global_device_ids=true | all-gather | bytes 737280 | tf_op jit(solution)/shard_map/all_gather | solution.py:20
  41.8 21.4 %psum.7 = f32[512]{0:T(512)S(1)} all-reduce(f32[512]{0:T(512)S(1)} %convert_reduce_fusion), channel_id=1, replica_groups=mesh['smp'=8,'par'=4] {'smp'}, use_global_device_ids=true, to_apply=%region_1.0 | all-reduce | flops 512 | bytes 4096 | tf_op jit(solution)/shard_map/psum | solution.py:11
  63.2 0.0 copy-done.1
  63.2 1.1 %convolution_bitcast_fusion = f32[640,80]{1,0:T(8,128)} fusion(bf16[640,512]{1,0:T(8,128)(2,1)S(1)} %all_gather.9, f32[512]{0:T(512)S(1)} %broadcast_multiply_fusion, bf16[80,512]{1,0:T(8,128)(2,1)S(1)} %copy-done.1), kind=kOutput, calls=%fused_computation.1 | convolution fusion | flops 53903360 | bytes 944128
  64.3 0.0 reduce-scatter.4.cloned.1.call-update
  64.3 0.0 copy-done
  64.3 0.2 convolution_bitcast_fusion.1
  64.5 26.1 %all-gather.1 = f32[8,1,512]{2,1,0:T(1,128)S(1)} all-gather(f32[1,1,512]{2,1,0:T(1,128)S(1)} %convolution_bitcast_fusion.1), channel_id=2, replica_groups=mesh['smp'=8,'par'=4] {'smp'}, dimensions={0}, use_global_device_ids=true | all-gather | bytes 18432 | tf_op jit(solution)/shard_map/all_gather | solution.py:25
  90.6 0.6 reduce_sum.19
  91.2 0.0 reduce-scatter.4.cloned.1.call-done
  91.2 1.6 %copy.5 = f32[80,160]{1,0:T(8,128)} copy(f32[80,160]{0,1:T(8,128)} %bitcast.10) | data formatting | bytes 102400
  (1 shorter events, 0.0 us)
Async XLA Ops:
  7.2 57.2 %copy-start = (f32[80]{0:T(128)S(1)}, f32[80]{0:T(128)}, u32[]{:S(2)}) copy-start(f32[80]{0:T(128)} %param.3) | copy-start | bytes 964
  7.2 56.1 %copy-start.1 = (bf16[80,512]{1,0:T(8,128)(2,1)S(1)}, bf16[80,512]{1,0:T(8,128)(2,1)}, u32[]{:S(2)}) copy-start(bf16[80,512]{1,0:T(8,128)(2,1)} %param.2) | copy-start | bytes 245764
  7.2 84.0 %reduce-scatter.4.cloned.1.call-start = ((), (), s32[]{:S(2)}) async-start(), calls=%async_computation.1 | async-start | bytes 409600
Sparse Core Ops, SparseCore 0:
  64.4 17.6 reduce-scatter.3
